TPU v7x, 32 devices: a whole 2x2x4 slice. The times are simulated.
32 devices in a mesh: groups: 2 (over y), ctx: 4 (over z), wt: 2 (over x), sub: 2 (over core).
Axes of the slice: x: 2, y: 2, z: 4, core: 2. Of those that a mesh axis runs over, the one named last changes fastest.
Arguments:
- queries: bfloat16 [16, 32, 128, 576], P(('groups', 'ctx'), None, ('wt', 'sub')), parts along dimension 0, may hold values from -80 to 80
- selection: int32 [16, 4, 2], P(('groups', 'ctx')), parts along dimension 0, may hold values from -1 to 15, as said below
- latent_cache: bfloat16 [128, 64, 576], P(('groups', 'ctx')), parts along dimension 0, may hold values from -8 to 8
- value_up: bfloat16 [128, 512, 128], P(None, ('wt', 'sub')), may hold values from -1 to 1
Outputs:
- attended: bfloat16 [16, 32, 128, 128], P(('groups', 'ctx'), None, ('wt', 'sub')), parts along dimension 0
There are 2 independent parts, one for each index of `groups`. A program takes and returns all parts, laid end to end along the dimension named above; an argument that names none is the same for every part. Nothing has to cross between parts.
Inputs may be any that keep to these rules, and one draw needn't show every extreme that they name: `selection`: entry [c, o, s] is the number of a block among the 16 of owner o, or -1 for an empty slot; in an owner's slots live entries come first and differ. Each query block has 4 live entries in all, and in every query block some owner fills all 2 slots.
All inputs are finite; a program needn't handle non-finite values.
Results may differ from a plain program's by a relative error of at most 0.008.
Values may be sent and summed in bfloat16 or wider, within the bound.
No kernel may reach another device: no remote copies, remote signals or barrier semaphores. Data moves between devices by JAX's collectives and lax.ppermute only.
A program may use at most 128 MiB of HBM per device.

v0:
```python
import jax
import jax.numpy as jnp
from jax import lax
from jax.sharding import PartitionSpec as P

LAT = 512
ROPE = 64
NOPE = 128


def attend(query, blocks, chosen):
    width = query.shape[2]
    owners = chosen.shape[0]
    count = chosen.shape[0] * chosen.shape[1]
    live = (chosen >= 0).reshape(-1)
    ranked = jnp.where(live, 0, count).astype(jnp.int32) + jnp.arange(count, dtype=jnp.int32)
    picked = jnp.argsort(ranked)[:owners]
    keys = blocks.reshape(count, blocks.shape[2], width)[picked].reshape(-1, width)
    rows = query.reshape(-1, width)
    scores = jnp.einsum("rd,kd->rk", rows, keys, preferred_element_type=jnp.float32)
    scores = scores * jnp.float32((NOPE + ROPE) ** (-0.5))
    expo = jnp.exp(scores - jnp.max(scores, axis=1, keepdims=True))
    totals = jnp.sum(expo, axis=1, keepdims=True)
    weights = expo.astype(jnp.bfloat16)
    latent = (jnp.dot(weights, keys[:, :LAT], preferred_element_type=jnp.float32) / totals).astype(
        jnp.bfloat16
    )
    return latent.reshape(query.shape[0], query.shape[1], LAT)


def per_device(queries, selection, latent_cache, value_up):
    owners = lax.axis_size("ctx")
    spans, per_span, heads_here, width = queries.shape
    slots = selection.shape[2]
    block_len = latent_cache.shape[1]

    def serve(asked):
        safe = jnp.clip(asked, 0, latent_cache.shape[0] - 1)
        return lax.all_to_all(latent_cache[safe], "ctx", split_axis=0, concat_axis=0, tiled=True)

    def fetch(wanted):
        half = slots // 2
        mine = lax.dynamic_slice_in_dim(wanted, lax.axis_index("sub") * half, half, 2)
        count = mine.shape[1] * mine.shape[2]
        fetched = serve(
            lax.all_to_all(
                mine.reshape(owners, count), "ctx", split_axis=0, concat_axis=0, tiled=True
            )
        )
        fetched = fetched.reshape(owners, mine.shape[1], mine.shape[2], block_len, width)
        fetched = lax.all_gather(fetched, "sub", axis=2, tiled=True)
        return fetched

    wanted_all = jnp.transpose(selection, (1, 0, 2))
    gathered = [fetch(wanted_all[:, index : index + 1])[:, 0] for index in range(spans)]
    latents = [attend(queries[index], gathered[index], selection[index]) for index in range(spans)]
    flat = jnp.stack(latents).reshape(spans * per_span, heads_here, LAT)
    my_weights = lax.all_to_all(value_up, ("wt", "sub"), split_axis=0, concat_axis=1, tiled=True)
    summed = jnp.einsum("nhl,hlv->nhv", flat, my_weights, preferred_element_type=jnp.float32)
    return summed.astype(jnp.bfloat16).reshape(spans, per_span, heads_here, my_weights.shape[2])


def solution(mesh):
    placed = (
        P(("groups", "ctx"), None, ("wt", "sub"), None),
        P(("groups", "ctx"), None, None),
        P(("groups", "ctx"), None, None),
        P(None, ("wt", "sub"), None),
    )
    return jax.shard_map(
        per_device,
        mesh=mesh,
        in_specs=placed,
        out_specs=P(("groups", "ctx"), None, ("wt", "sub"), None),
        check_vma=False,
    )
```

profile of v0, /device:TPU:0, one launch (start us, length us, event | category | flops | bytes accessed | tf_op | source)
XLA Modules:
  0.0 102.0 jit_solution(10457877809274622)
XLA Ops:
  0.0 0.0 copy-start
  0.0 0.9 copy.21
  0.9 0.7 constant_dynamic-slice_fusion.1
  1.6 6.3 %all-to-all-start = ((s32[4,1,1]{2,1,0:T(1,128)}), s32[4,1,1]{2,1,0:T(1,128)S(1)}, u32[]{:S(2)}, u32[]{:S(2)}) async-start(s32[4,1,1]{2,1,0:T(1,128)} %constant_dynamic-slice_fusion.1), calls=%async_computation | async-start | bytes 4096 | tf_op jit(solution)/shard_map/all_to_all | solution.py:46
  7.9 0.7 constant_dynamic-slice_fusion
  8.6 4.8 %all-to-all-done = s32[4,1,1]{2,1,0:T(1,128)S(1)} async-done(((s32[4,1,1]{2,1,0:T(1,128)}), s32[4,1,1]{2,1,0:T(1,128)S(1)}, u32[]{:S(2)}, u32[]{:S(2)}) %all-to-all-start) | async-done | bytes 48 | tf_op jit(solution)/shard_map/all_to_all | solution.py:46
  13.3 3.2 %all-to-all-start.2 = ((s32[4,1,1]{2,1,0:T(1,128)}), s32[4,1,1]{2,1,0:T(1,128)S(1)}, u32[]{:S(2)}, u32[]{:S(2)}) async-start(s32[4,1,1]{2,1,0:T(1,128)} %constant_dynamic-slice_fusion), calls=%async_computation.2 | async-start | bytes 4096 | tf_op jit(solution)/shard_map/all_to_all | solution.py:46
  16.6 0.2 fusion.10
  16.7 0.0 copy-done
  16.7 1.3 %gather_fusion = bf16[4,64,576]{2,1,0:T(8,128)(2,1)} fusion(bf16[16,64,576]{2,1,0:T(8,128)(2,1)S(1)} %copy-done, s32[1024]{0:T(1024)S(1)} %pad_clamp_fusion.3), kind=kCustom, calls=%fused_computation | custom fusion | bytes 589840 | tf_op jit(solution)/shard_map/gather | solution.py:39
  18.0 4.0 %all-to-all-done.2 = s32[4,1,1]{2,1,0:T(1,128)S(1)} async-done(((s32[4,1,1]{2,1,0:T(1,128)}), s32[4,1,1]{2,1,0:T(1,128)S(1)}, u32[]{:S(2)}, u32[]{:S(2)}) %all-to-all-start.2) | async-done | bytes 48 | tf_op jit(solution)/shard_map/all_to_all | solution.py:46
  22.0 3.5 %all-to-all-start.1 = ((bf16[4,1,64,576]{3,2,1,0:T(8,128)(2,1)}), bf16[4,1,64,576]{3,2,1,0:T(8,128)(2,1)S(1)}, u32[]{:S(2)}, u32[]{:S(2)}) async-start(bf16[4,1,64,576]{3,2,1,0:T(8,128)(2,1)} %bitcast.1), calls=%async_computation.1 | async-start | bytes 655360 | tf_op jit(solution)/shard_map/all_to_all | solution.py:39
  25.5 0.2 fusion.11
  25.7 1.3 %gather_fusion.2 = bf16[4,64,576]{2,1,0:T(8,128)(2,1)} fusion(bf16[16,64,576]{2,1,0:T(8,128)(2,1)S(1)} %copy-done, s32[1024]{0:T(1024)S(1)} %pad_clamp_fusion.1), kind=kCustom, calls=%fused_computation.2 | custom fusion | bytes 589840 | tf_op jit(solution)/shard_map/gather | solution.py:39
  27.0 5.8 %all-to-all-done.1 = bf16[4,1,64,576]{3,2,1,0:T(8,128)(2,1)S(1)} async-done(((bf16[4,1,64,576]{3,2,1,0:T(8,128)(2,1)}), bf16[4,1,64,576]{3,2,1,0:T(8,128)(2,1)S(1)}, u32[]{:S(2)}, u32[]{:S(2)}) %all-to-all-start.1) | async-done | bytes 294944 | tf_op jit(solution)/shard_map/all_to_all | solution.py:39
  32.8 3.6 %all-to-all-start.3 = ((bf16[4,1,64,576]{3,2,1,0:T(8,128)(2,1)}), bf16[4,1,64,576]{3,2,1,0:T(8,128)(2,1)S(1)}, u32[]{:S(2)}, u32[]{:S(2)}) async-start(bf16[4,1,64,576]{3,2,1,0:T(8,128)(2,1)} %bitcast.6), calls=%async_computation.3 | async-start | bytes 655360 | tf_op jit(solution)/shard_map/all_to_all | solution.py:39
  36.4 0.1 copy.22
  36.5 0.1 select_n.38
  36.5 0.1 copy.23
  36.6 0.1 select_n.42
  36.7 6.9 %all-to-all-done.3 = bf16[4,1,64,576]{3,2,1,0:T(8,128)(2,1)S(1)} async-done(((bf16[4,1,64,576]{3,2,1,0:T(8,128)(2,1)}), bf16[4,1,64,576]{3,2,1,0:T(8,128)(2,1)S(1)}, u32[]{:S(2)}, u32[]{:S(2)}) %all-to-all-start.3) | async-done | bytes 294944 | tf_op jit(solution)/shard_map/all_to_all | solution.py:39
  43.7 0.0 copy-done.1
  43.7 0.7 copy-done.2
  44.4 4.9 %all-to-all-start.4 = ((bf16[128,128,128]{2,1,0:T(8,128)(2,1)}), bf16[128,128,128]{2,1,0:T(8,128)(2,1)}, u32[]{:S(2)}, u32[]{:S(2)}) async-start(bf16[128,128,128]{2,1,0:T(8,128)(2,1)} %param.7), calls=%async_computation.4 | async-start | bytes 8388608 | tf_op jit(solution)/shard_map/all_to_all | solution.py:58
  49.3 1.0 sort.31
  50.2 1.0 sort.32
  51.3 0.0 copy-start.3
  51.3 3.1 %fusion.12 = (bf16[1,32,32,576]{3,2,1,0:T(8,128)(2,1)S(1)}, bf16[1,32,32,576]{3,2,1,0:T(8,128)(2,1)}) fusion(bf16[2,32,32,576]{3,2,1,0:T(8,128)(2,1)} %param.4), kind=kLoop, calls=%fused_computation.36 | loop fusion | bytes 4718592 | tf_op jit(solution)/shard_map/slice | solution.py:56
  54.4 0.0 copy-done.3
  54.4 2.3 %all-gather.1 = bf16[4,2,64,576]{3,2,1,0:T(8,128)(2,1)S(1)} all-gather(bf16[4,1,64,576]{3,2,1,0:T(8,128)(2,1)S(1)} %copy-done.3), channel_id=3, replica_groups=mesh['groups'=2,'ctx'=4,'wt'=2,'sub'=2] {'sub'}, dimensions={1}, use_global_device_ids=true | all-gather | bytes 884736 | tf_op jit(solution)/shard_map/all_gather | solution.py:51
  56.7 1.3 %gather_fusion.3 = bf16[4,64,576]{2,1,0:T(8,128)(2,1)} fusion(bf16[8,64,576]{2,1,0:T(8,128)(2,1)S(1)} %bitcast.30, s32[1024]{0:T(1024)S(1)} %pad_clamp_fusion), kind=kCustom, calls=%fused_computation.3 | custom fusion | bytes 589840 | tf_op jit(solution)/shard_map/gather | solution.py:18
  58.0 2.5 %all-gather = bf16[4,2,64,576]{3,2,1,0:T(8,128)(2,1)S(1)} all-gather(bf16[4,1,64,576]{3,2,1,0:T(8,128)(2,1)} %copy-done.1), channel_id=2, replica_groups=mesh['groups'=2,'ctx'=4,'wt'=2,'sub'=2] {'sub'}, dimensions={1}, use_global_device_ids=true | all-gather | bytes 884736 | tf_op jit(solution)/shard_map/all_gather | solution.py:51
  60.5 1.3 %gather_fusion.1 = bf16[4,64,576]{2,1,0:T(8,128)(2,1)} fusion(bf16[8,64,576]{2,1,0:T(8,128)(2,1)S(1)} %bitcast.31, s32[1024]{0:T(1024)S(1)} %pad_clamp_fusion.2), kind=kCustom, calls=%fused_computation.1 | custom fusion | bytes 589840 | tf_op jit(solution)/shard_map/gather | solution.py:18
  61.8 2.1 %fusion.14 = (f32[1024]{0:T(1024)S(1)}, f32[256,1024]{1,0:T(8,128)S(1)}) fusion(bf16[256,576]{1,0:T(8,128)(2,1)} %bitcast.32, bf16[1024,576]{1,0:T(8,128)(2,1)} %bitcast.28), kind=kOutput, calls=%fused_computation.38 | convolution fusion | flops 302513152 | bytes 2527232 | tf_op jit(solution)/shard_map/rd,kd->rk/dot_general | solution.py:20
  63.9 0.2 fusion.2
  64.1 0.0 copy-start.4
  64.1 0.0 copy-done.5
  64.1 0.6 fusion.15
  64.7 0.2 fusion
  64.9 0.1 copy-done.4
  65.0 0.5 divide_convert_fusion
  65.5 0.5 divide_convert_fusion.1
  66.1 0.2 pad_maximum_fusion
  66.3 1.2 %copy.24 = bf16[2,32,32,512]{3,1,0,2:T(8,128)(2,1)S(1)} copy(bf16[2,32,32,512]{3,2,1,0:T(8,128)(2,1)S(1)} %pad_maximum_fusion) | data formatting | bytes 4194304 | tf_op jit(solution)/shard_map/stack | solution.py:57
  67.4 30.0 %all-to-all-done.4 = bf16[128,128,128]{2,1,0:T(8,128)(2,1)} async-done(((bf16[128,128,128]{2,1,0:T(8,128)(2,1)}), bf16[128,128,128]{2,1,0:T(8,128)(2,1)}, u32[]{:S(2)}, u32[]{:S(2)}) %all-to-all-start.4) | async-done | bytes 4194336 | tf_op jit(solution)/shard_map/all_to_all | solution.py:58
  97.5 2.5 %copy.25 = bf16[4,32,128,128]{3,2,0,1:T(8,128)(2,1)S(1)} copy(bf16[4,32,128,128]{3,2,1,0:T(8,128)(2,1)} %bitcast.12) | data formatting | bytes 8388608 | tf_op jit(solution)/shard_map/all_to_all | solution.py:58
  100.0 0.9 convolution_convert_fusion
  100.8 1.1 %copy.26 = bf16[2,32,32,128]{3,2,1,0:T(8,128)(2,1)} copy(bf16[2,32,32,128]{3,1,0,2:T(8,128)(2,1)S(1)} %bitcast.29) | data formatting | bytes 1048576 | tf_op jit(solution)/shard_map/reshape | solution.py:60
  (17 shorter events, 0.1 us)
Async XLA Ops:
  0.0 16.7 %copy-start = (bf16[16,64,576]{2,1,0:T(8,128)(2,1)S(1)}, bf16[16,64,576]{2,1,0:T(8,128)(2,1)}, u32[]{:S(2)}) copy-start(bf16[16,64,576]{2,1,0:T(8,128)(2,1)} %param.6) | copy-start | bytes 3538948
  0.0 36.4 %copy-start.6 = (s32[2,4,2]{1,2,0:T(2,128)S(1)}, s32[2,4,2]{1,2,0:T(2,128)}, u32[]{:S(2)}) copy-start(s32[2,4,2]{1,2,0:T(2,128)} %param.5) | copy-start | bytes 196
  1.6 11.8 %all-to-all-start = ((s32[4,1,1]{2,1,0:T(1,128)}), s32[4,1,1]{2,1,0:T(1,128)S(1)}, u32[]{:S(2)}, u32[]{:S(2)}) async-start(s32[4,1,1]{2,1,0:T(1,128)} %constant_dynamic-slice_fusion.1), calls=%async_computation | async-start | bytes 4096 | tf_op jit(solution)/shard_map/all_to_all | solution.py:46
  13.3 8.7 %all-to-all-start.2 = ((s32[4,1,1]{2,1,0:T(1,128)}), s32[4,1,1]{2,1,0:T(1,128)S(1)}, u32[]{:S(2)}, u32[]{:S(2)}) async-start(s32[4,1,1]{2,1,0:T(1,128)} %constant_dynamic-slice_fusion), calls=%async_computation.2 | async-start | bytes 4096 | tf_op jit(solution)/shard_map/all_to_all | solution.py:46
  22.0 10.7 %all-to-all-start.1 = ((bf16[4,1,64,576]{3,2,1,0:T(8,128)(2,1)}), bf16[4,1,64,576]{3,2,1,0:T(8,128)(2,1)S(1)}, u32[]{:S(2)}, u32[]{:S(2)}) async-start(bf16[4,1,64,576]{3,2,1,0:T(8,128)(2,1)} %bitcast.1), calls=%async_computation.1 | async-start | bytes 655360 | tf_op jit(solution)/shard_map/all_to_all | solution.py:39
  32.8 10.9 %copy-start.1 = (bf16[4,1,64,576]{3,2,1,0:T(8,128)(2,1)}, bf16[4,1,64,576]{3,2,1,0:T(8,128)(2,1)S(1)}, u32[]{:S(2)}) copy-start(bf16[4,1,64,576]{3,2,1,0:T(8,128)(2,1)S(1)} %all-to-all-done.1) | copy-start | bytes 884740
  32.8 10.9 %all-to-all-start.3 = ((bf16[4,1,64,576]{3,2,1,0:T(8,128)(2,1)}), bf16[4,1,64,576]{3,2,1,0:T(8,128)(2,1)S(1)}, u32[]{:S(2)}, u32[]{:S(2)}) async-start(bf16[4,1,64,576]{3,2,1,0:T(8,128)(2,1)} %bitcast.6), calls=%async_computation.3 | async-start | bytes 655360 | tf_op jit(solution)/shard_map/all_to_all | solution.py:39
  43.7 0.7 copy-start.2
  44.4 53.1 %all-to-all-start.4 = ((bf16[128,128,128]{2,1,0:T(8,128)(2,1)}), bf16[128,128,128]{2,1,0:T(8,128)(2,1)}, u32[]{:S(2)}, u32[]{:S(2)}) async-start(bf16[128,128,128]{2,1,0:T(8,128)(2,1)} %param.7), calls=%async_computation.4 | async-start | bytes 8388608 | tf_op jit(solution)/shard_map/all_to_all | solution.py:58
  51.3 3.1 %copy-start.3 = (bf16[4,1,64,576]{3,2,1,0:T(8,128)(2,1)S(1)}, bf16[4,1,64,576]{3,2,1,0:T(8,128)(2,1)}, u32[]{:S(2)}) copy-start(bf16[4,1,64,576]{3,2,1,0:T(8,128)(2,1)} %copy-done.2) | copy-start | bytes 884740
  61.8 2.3 %copy-start.5 = (bf16[4,64,576]{2,1,0:T(8,128)(2,1)S(1)}, bf16[4,64,576]{2,1,0:T(8,128)(2,1)}, u32[]{:S(2)}) copy-start(bf16[4,64,576]{2,1,0:T(8,128)(2,1)} %gather_fusion.1) | copy-start | bytes 884740
  64.1 1.0 copy-start.4
where the time goes:
time: 103 us; the launch traced here: 102 us
  waiting for transfers between devices  51.5 us (50%)
  starting transfers between devices  21.5 us (21%)
  local copies, waits for them, and re-layouts  16.6 us (16%)
  blocking collectives  4.81 us (5%)
  matrix products  4.57 us (4%)
  other arithmetic  2.85 us (3%)
    all_to_all x1, waiting for transfers between devices, per_device(): lax.all_to_all(value_up, ('wt', 'sub'), split_axis=0, concat_axis=1, tile...  30 us
    all_to_all x2, waiting for transfers between devices, serve(): lax.all_to_all(latent_cache[safe], 'ctx', split_axis=0, concat_axis=0, ti...  12.7 us
    all_to_all x2, starting transfers between devices, fetch(): lax.all_to_all(mine.reshape(owners, count), 'ctx', split_axis=0, concat_a...  9.57 us
    all_to_all x2, waiting for transfers between devices, fetch(): lax.all_to_all(mine.reshape(owners, count), 'ctx', split_axis=0, concat_a...  8.76 us
    all_to_all x2, starting transfers between devices, serve(): lax.all_to_all(latent_cache[safe], 'ctx', split_axis=0, concat_axis=0, ti...  7.06 us
    all_to_all x1, starting transfers between devices, per_device(): lax.all_to_all(value_up, ('wt', 'sub'), split_axis=0, concat_axis=1, tile...  4.86 us
    all_gather x2, blocking collectives, fetch(): fetched = lax.all_gather(fetched, 'sub', axis=2, tiled=True)  4.81 us
    slice x1, local copies, waits for them, and re-layouts, per_device(): queries[index]  3.08 us
  transfers between devices with their start and end apart: 5, of which 5 were waited for; matrix products, arithmetic and copies ran while one was open for 17% of the time, Pallas kernels for 0%

commit v1 on v0

--- a/solution.py
+++ b/solution.py
@@ -1,3 +1,4 @@
+import functools
 import jax
 import jax.numpy as jnp
 from jax import lax
@@ -6,6 +7,27 @@
 LAT = 512
 ROPE = 64
 NOPE = 128
+
+
+def threads_time(vec, group_axis):
+    parts_out = lax.axis_size(group_axis)
+    arr_now = lax.axis_index(group_axis)
+    moved, oldest = (parts_out, arr_now)
+    all_rows = vec.shape[0] // moved
+    all_values = jnp.roll(vec, -oldest * all_rows, axis=0)
+    lanes = [lax.slice_in_dim(all_values, 0, all_rows, axis=0)]
+    for t in range(1, moved):
+        w_next = lax.slice_in_dim(all_values, t * all_rows, (t + 1) * all_rows, axis=0)
+        lanes.append(
+            lax.ppermute(
+                w_next, group_axis, [(dev_i, (dev_i + t) % moved) for dev_i in range(moved)]
+            )
+        )
+    low = jnp.concatenate(lanes[::-1], axis=0)
+    return jnp.roll(low, (oldest + 1) * lanes[0].shape[0], axis=0)
+
+
+_supply_leaf = functools.partial(threads_time, group_axis="ctx")
 
 
 def attend(query, blocks, chosen):
@@ -42,11 +64,7 @@
         half = slots // 2
         mine = lax.dynamic_slice_in_dim(wanted, lax.axis_index("sub") * half, half, 2)
         count = mine.shape[1] * mine.shape[2]
-        fetched = serve(
-            lax.all_to_all(
-                mine.reshape(owners, count), "ctx", split_axis=0, concat_axis=0, tiled=True
-            )
-        )
+        fetched = serve(_supply_leaf(mine.reshape(owners, count)))
         fetched = fetched.reshape(owners, mine.shape[1], mine.shape[2], block_len, width)
         fetched = lax.all_gather(fetched, "sub", axis=2, tiled=True)
         return fetched

time: 103 us -> 105 us (1.019)
  waiting for transfers between devices: 51.5 us -> 45.7 us
  other arithmetic: 2.85 us -> 7.87 us
  starting transfers between devices: 21.5 us -> 24.3 us
    ppermute x0 -> x6, starting transfers between devices: none -> 11 us  [threads_time(): lax.ppermute(w_next, group_axis, [(dev_i, (dev_i + t) % moved) for dev_i...]
    all_to_all x2 -> x0, starting transfers between devices: 9.57 us -> none  [fetch(): lax.all_to_all(mine.reshape(owners, count), 'ctx', split_axis=0, concat_a...]
    ppermute x0 -> x6, waiting for transfers between devices: none -> 8.77 us  [threads_time(): lax.ppermute(w_next, group_axis, [(dev_i, (dev_i + t) % moved) for dev_i...]
    all_to_all x2 -> x0, waiting for transfers between devices: 8.76 us -> none  [fetch(): lax.all_to_all(mine.reshape(owners, count), 'ctx', split_axis=0, concat_a...]
    all_to_all x2, waiting for transfers between devices: 12.7 us -> 6.94 us  [serve(): lax.all_to_all(latent_cache[safe], 'ctx', split_axis=0, concat_axis=0, ti...]
    concatenate x0 -> x4, other arithmetic: none -> 5.19 us  [the longest x2 5.04 us: threads_time(): return jnp.roll(low, (oldest + 1) * lanes[0].shape[0], axis=0)]
    all_to_all x2, starting transfers between devices: 7.06 us -> 8.38 us  [serve(): lax.all_to_all(latent_cache[safe], 'ctx', split_axis=0, concat_axis=0, ti...]
    slice x0 -> x2, local copies, waits for them, and re-layouts: none -> 1.28 us  [threads_time(): lax.slice_in_dim(all_values, t * all_rows, (t + 1) * all_rows, axis=0)]
  transfers between devices with their start and end apart: 5 -> 9, of which waited for: 5 -> 6; matrix products, arithmetic and copies ran while one was open for 17% -> 17% of each run, Pallas kernels for 0% -> 0%
where the time goes in v1:
time: 105 us; the launch traced here: 104 us
  waiting for transfers between devices  45.7 us (44%)
  starting transfers between devices  24.3 us (23%)
  local copies, waits for them, and re-layouts  16.6 us (16%)
  other arithmetic  7.87 us (7%)
  blocking collectives  4.81 us (5%)
  matrix products  4.56 us (4%)
    all_to_all x1, waiting for transfers between devices, per_device(): lax.all_to_all(value_up, ('wt', 'sub'), split_axis=0, concat_axis=1, tile...  30 us
    ppermute x6, starting transfers between devices, threads_time(): lax.ppermute(w_next, group_axis, [(dev_i, (dev_i + t) % moved) for dev_i...  11 us
    ppermute x6, waiting for transfers between devices, threads_time(): lax.ppermute(w_next, group_axis, [(dev_i, (dev_i + t) % moved) for dev_i...  8.77 us
    all_to_all x2, starting transfers between devices, serve(): lax.all_to_all(latent_cache[safe], 'ctx', split_axis=0, concat_axis=0, ti...  8.38 us
    all_to_all x2, waiting for transfers between devices, serve(): lax.all_to_all(latent_cache[safe], 'ctx', split_axis=0, concat_axis=0, ti...  6.94 us
    concatenate x2, other arithmetic, threads_time(): return jnp.roll(low, (oldest + 1) * lanes[0].shape[0], axis=0)  5.04 us
    all_to_all x1, starting transfers between devices, per_device(): lax.all_to_all(value_up, ('wt', 'sub'), split_axis=0, concat_axis=1, tile...  4.86 us
    all_gather x2, blocking collectives, fetch(): fetched = lax.all_gather(fetched, 'sub', axis=2, tiled=True)  4.81 us
  transfers between devices with their start and end apart: 9, of which 6 were waited for; matrix products, arithmetic and copies ran while one was open for 17% of the time, Pallas kernels for 0%

profile of v1, /device:TPU:0, one launch (start us, length us, event | category | flops | bytes accessed | tf_op | source)
XLA Modules:
  0.0 104.1 jit_solution(8502659693356152239)
XLA Ops:
  0.0 0.8 fusion.17
  0.8 0.1 pad_add_fusion.1
  0.9 0.1 constant_dynamic-slice_fusion
  1.0 0.6 fusion.19
  1.6 5.1 %collective-permute-start.3 = (s32[1,1]{0,1:T(1,128)}, s32[1,1]{0,1:T(1,128)}, u32[]{:S(2)}, u32[]{:S(2)}) collective-permute-start(s32[1,1]{0,1:T(1,128)} %get-tuple-element.20), channel_id=1, source_target_pairs={{0,12},{4,0},{8,4},{12,8},{1,13},{5,1},{9,5},{13,9},{2,14},{6,2},{... | collective-permute-start | bytes 20 | tf_op jit(solution)/shard_map/ppermute | solution.py:22
  6.7 1.0 collective-permute-start.4
  7.8 0.3 collective-permute-done.3
  8.1 4.1 %collective-permute-done.5 = s32[1,1]{0,1:T(1,128)} collective-permute-done((s32[1,1]{0,1:T(1,128)}, s32[1,1]{0,1:T(1,128)}, u32[]{:S(2)}, u32[]{:S(2)}) %collective-permute-start.5) | collective-permute-done | bytes 36 | tf_op jit(solution)/shard_map/ppermute | solution.py:22
  12.2 2.6 %add_add_fusion.1 = s32[8,1]{0,1:T(1,128)S(1)} fusion(s32[1,1]{0,1:T(1,128)} %get-tuple-element.21, s32[1,1]{0,1:T(1,128)} %collective-permute-done.5, s32[1,1]{0,1:T(1,128)} %collective-permute-done.4, s32[1,1]{0,1:T(1,128)} %collective-permute-done.3), kind=kLoop, calls=%fused_computation.43 | loop fusion | flops 56 | bytes 48 | tf_op jit(solution)/shard_map/jit(_roll_dynamic)/concatenate | solution.py:27
  14.8 0.1 fusion.15
  14.9 1.3 %gather_fusion.2 = bf16[4,64,576]{2,1,0:T(8,128)(2,1)} fusion(bf16[16,64,576]{2,1,0:T(8,128)(2,1)S(1)} %copy-done, s32[1024]{0:T(1024)S(1)} %pad_clamp_fusion.1), kind=kCustom, calls=%fused_computation.2 | custom fusion | bytes 589840 | tf_op jit(solution)/shard_map/gather | solution.py:61
  16.2 4.2 %all-to-all-start.1 = ((bf16[4,1,64,576]{3,2,1,0:T(8,128)(2,1)}), bf16[4,1,64,576]{3,2,1,0:T(8,128)(2,1)S(1)}, u32[]{:S(2)}, u32[]{:S(2)}) async-start(bf16[4,1,64,576]{3,2,1,0:T(8,128)(2,1)} %bitcast.10), calls=%async_computation.1 | async-start | bytes 655360 | tf_op jit(solution)/shard_map/all_to_all | solution.py:61
  20.4 0.7 fusion.18
  21.1 3.8 %collective-permute-start = (s32[1,1]{0,1:T(1,128)}, s32[1,1]{0,1:T(1,128)}, u32[]{:S(2)}, u32[]{:S(2)}) collective-permute-start(s32[1,1]{0,1:T(1,128)} %get-tuple-element.16), channel_id=1, source_target_pairs={{0,12},{4,0},{8,4},{12,8},{1,13},{5,1},{9,5},{13,9},{2,14},{6,2},{... | collective-permute-start | bytes 20 | tf_op jit(solution)/shard_map/ppermute | solution.py:22
  24.9 1.1 %collective-permute-start.1 = (s32[1,1]{0,1:T(1,128)}, s32[1,1]{0,1:T(1,128)}, u32[]{:S(2)}, u32[]{:S(2)}) collective-permute-start(s32[1,1]{0,1:T(1,128)} %get-tuple-element.19), channel_id=1, source_target_pairs={{0,8},{4,12},{8,0},{12,4},{1,9},{5,13},{9,1},{13,5},{2,10},{6,14},... | collective-permute-start | bytes 20 | tf_op jit(solution)/shard_map/ppermute | solution.py:22
  26.0 0.2 collective-permute-done
  26.3 4.2 %collective-permute-done.2 = s32[1,1]{0,1:T(1,128)} collective-permute-done((s32[1,1]{0,1:T(1,128)}, s32[1,1]{0,1:T(1,128)}, u32[]{:S(2)}, u32[]{:S(2)}) %collective-permute-start.2) | collective-permute-done | bytes 36 | tf_op jit(solution)/shard_map/ppermute | solution.py:22
  30.4 2.4 %add_add_fusion = s32[8,1]{0,1:T(1,128)S(1)} fusion(s32[1,1]{0,1:T(1,128)} %get-tuple-element.17, s32[1,1]{0,1:T(1,128)} %collective-permute-done.2, s32[1,1]{0,1:T(1,128)} %collective-permute-done.1, s32[1,1]{0,1:T(1,128)} %collective-permute-done), kind=kLoop, calls=%fused_computation.41 | loop fusion | flops 56 | bytes 48 | tf_op jit(solution)/shard_map/jit(_roll_dynamic)/concatenate | solution.py:27
  32.9 0.1 fusion.14
  32.9 1.3 %gather_fusion = bf16[4,64,576]{2,1,0:T(8,128)(2,1)} fusion(bf16[16,64,576]{2,1,0:T(8,128)(2,1)S(1)} %copy-done, s32[1024]{0:T(1024)S(1)} %pad_clamp_fusion.3), kind=kCustom, calls=%fused_computation | custom fusion | bytes 589840 | tf_op jit(solution)/shard_map/gather | solution.py:61
  34.2 4.2 %all-to-all-start = ((bf16[4,1,64,576]{3,2,1,0:T(8,128)(2,1)}), bf16[4,1,64,576]{3,2,1,0:T(8,128)(2,1)S(1)}, u32[]{:S(2)}, u32[]{:S(2)}) async-start(bf16[4,1,64,576]{3,2,1,0:T(8,128)(2,1)} %bitcast.3), calls=%async_computation | async-start | bytes 655360 | tf_op jit(solution)/shard_map/all_to_all | solution.py:61
  38.5 0.1 copy.10
  38.5 0.1 select_n.42
  38.6 0.1 copy.11
  38.7 0.1 select_n.46
  38.8 6.9 %all-to-all-done = bf16[4,1,64,576]{3,2,1,0:T(8,128)(2,1)S(1)} async-done(((bf16[4,1,64,576]{3,2,1,0:T(8,128)(2,1)}), bf16[4,1,64,576]{3,2,1,0:T(8,128)(2,1)S(1)}, u32[]{:S(2)}, u32[]{:S(2)}) %all-to-all-start) | async-done | bytes 294944 | tf_op jit(solution)/shard_map/all_to_all | solution.py:61
  45.7 0.7 copy-done.2
  46.5 4.9 %all-to-all-start.2 = ((bf16[128,128,128]{2,1,0:T(8,128)(2,1)}), bf16[128,128,128]{2,1,0:T(8,128)(2,1)}, u32[]{:S(2)}, u32[]{:S(2)}) async-start(bf16[128,128,128]{2,1,0:T(8,128)(2,1)} %param.9), calls=%async_computation.2 | async-start | bytes 8388608 | tf_op jit(solution)/shard_map/all_to_all | solution.py:76
  51.4 1.0 sort.31
  52.4 1.0 sort.32
  53.4 3.1 %fusion.16 = (bf16[1,32,32,576]{3,2,1,0:T(8,128)(2,1)S(1)}, bf16[1,32,32,576]{3,2,1,0:T(8,128)(2,1)}) fusion(bf16[2,32,32,576]{3,2,1,0:T(8,128)(2,1)} %param.6), kind=kLoop, calls=%fused_computation.48 | loop fusion | bytes 4718592 | tf_op jit(solution)/shard_map/slice | solution.py:74
  56.5 2.3 %all-gather = bf16[4,2,64,576]{3,2,1,0:T(8,128)(2,1)S(1)} all-gather(bf16[4,1,64,576]{3,2,1,0:T(8,128)(2,1)S(1)} %copy-done.3), channel_id=2, replica_groups=mesh['groups'=2,'ctx'=4,'wt'=2,'sub'=2] {'sub'}, dimensions={1}, use_global_device_ids=true | all-gather | bytes 884736 | tf_op jit(solution)/shard_map/all_gather | solution.py:69
  58.8 1.3 %gather_fusion.1 = bf16[4,64,576]{2,1,0:T(8,128)(2,1)} fusion(bf16[8,64,576]{2,1,0:T(8,128)(2,1)S(1)} %bitcast.38, s32[1024]{0:T(1024)S(1)} %pad_clamp_fusion.2), kind=kCustom, calls=%fused_computation.1 | custom fusion | bytes 589840 | tf_op jit(solution)/shard_map/gather | solution.py:40
  60.1 2.5 %all-gather.1 = bf16[4,2,64,576]{3,2,1,0:T(8,128)(2,1)S(1)} all-gather(bf16[4,1,64,576]{3,2,1,0:T(8,128)(2,1)} %copy-done.1), channel_id=3, replica_groups=mesh['groups'=2,'ctx'=4,'wt'=2,'sub'=2] {'sub'}, dimensions={1}, use_global_device_ids=true | all-gather | bytes 884736 | tf_op jit(solution)/shard_map/all_gather | solution.py:69
  62.6 1.3 %gather_fusion.3 = bf16[4,64,576]{2,1,0:T(8,128)(2,1)} fusion(bf16[8,64,576]{2,1,0:T(8,128)(2,1)S(1)} %bitcast.39, s32[1024]{0:T(1024)S(1)} %pad_clamp_fusion), kind=kCustom, calls=%fused_computation.3 | custom fusion | bytes 589840 | tf_op jit(solution)/shard_map/gather | solution.py:40
  63.9 2.1 %fusion.20 = (f32[1024]{0:T(1024)S(1)}, f32[256,1024]{1,0:T(8,128)S(1)}) fusion(bf16[256,576]{1,0:T(8,128)(2,1)} %bitcast.42, bf16[1024,576]{1,0:T(8,128)(2,1)} %bitcast.36), kind=kOutput, calls=%fused_computation.52 | convolution fusion | flops 302513152 | bytes 2527232 | tf_op jit(solution)/shard_map/rd,kd->rk/dot_general | solution.py:42
  66.0 0.2 fusion.2
  66.2 0.6 fusion.21
  66.8 0.2 fusion
  67.0 0.1 copy-done.5
  67.2 0.5 divide_convert_fusion
  67.7 0.5 divide_convert_fusion.1
  68.2 0.2 pad_maximum_fusion
  68.4 1.2 %copy.12 = bf16[2,32,32,512]{3,1,0,2:T(8,128)(2,1)S(1)} copy(bf16[2,32,32,512]{3,2,1,0:T(8,128)(2,1)S(1)} %pad_maximum_fusion) | data formatting | bytes 4194304 | tf_op jit(solution)/shard_map/stack | solution.py:75
  69.5 30.0 %all-to-all-done.2 = bf16[128,128,128]{2,1,0:T(8,128)(2,1)} async-done(((bf16[128,128,128]{2,1,0:T(8,128)(2,1)}), bf16[128,128,128]{2,1,0:T(8,128)(2,1)}, u32[]{:S(2)}, u32[]{:S(2)}) %all-to-all-start.2) | async-done | bytes 4194336 | tf_op jit(solution)/shard_map/all_to_all | solution.py:76
  99.6 2.5 %copy.13 = bf16[4,32,128,128]{3,2,0,1:T(8,128)(2,1)S(1)} copy(bf16[4,32,128,128]{3,2,1,0:T(8,128)(2,1)} %bitcast.16) | data formatting | bytes 8388608 | tf_op jit(solution)/shard_map/all_to_all | solution.py:76
  102.1 0.9 convolution_convert_fusion
  102.9 1.1 %copy.14 = bf16[2,32,32,128]{3,2,1,0:T(8,128)(2,1)} copy(bf16[2,32,32,128]{3,1,0,2:T(8,128)(2,1)S(1)} %bitcast.37) | data formatting | bytes 1048576 | tf_op jit(solution)/shard_map/reshape | solution.py:78
  (31 shorter events, 0.2 us)
Async XLA Ops:
  0.0 14.9 %copy-start = (bf16[16,64,576]{2,1,0:T(8,128)(2,1)S(1)}, bf16[16,64,576]{2,1,0:T(8,128)(2,1)}, u32[]{:S(2)}) copy-start(bf16[16,64,576]{2,1,0:T(8,128)(2,1)} %param.8) | copy-start | bytes 3538948
  0.0 38.4 %copy-start.6 = (s32[2,4,2]{1,2,0:T(2,128)S(1)}, s32[2,4,2]{1,2,0:T(2,128)}, u32[]{:S(2)}) copy-start(s32[2,4,2]{1,2,0:T(2,128)} %param.7) | copy-start | bytes 196
  1.6 6.5 %collective-permute-start.3 = (s32[1,1]{0,1:T(1,128)}, s32[1,1]{0,1:T(1,128)}, u32[]{:S(2)}, u32[]{:S(2)}) collective-permute-start(s32[1,1]{0,1:T(1,128)} %get-tuple-element.20), channel_id=1, source_target_pairs={{0,12},{4,0},{8,4},{12,8},{1,13},{5,1},{9,5},{13,9},{2,14},{6,2},{... | collective-permute-start | bytes 20 | tf_op jit(solution)/shard_map/ppermute | solution.py:22
  6.7 5.5 %collective-permute-start.5 = (s32[1,1]{0,1:T(1,128)}, s32[1,1]{0,1:T(1,128)}, u32[]{:S(2)}, u32[]{:S(2)}) collective-permute-start(s32[1,1]{0,1:T(1,128)} %get-tuple-element.22), channel_id=1, source_target_pairs={{0,4},{4,8},{8,12},{12,0},{1,5},{5,9},{9,13},{13,1},{2,6},{6,10},{... | collective-permute-start | bytes 20 | tf_op jit(solution)/shard_map/ppermute | solution.py:22
  6.7 5.5 %collective-permute-start.4 = (s32[1,1]{0,1:T(1,128)}, s32[1,1]{0,1:T(1,128)}, u32[]{:S(2)}, u32[]{:S(2)}) collective-permute-start(s32[1,1]{0,1:T(1,128)} %get-tuple-element.23), channel_id=1, source_target_pairs={{0,8},{4,12},{8,0},{12,4},{1,9},{5,13},{9,1},{13,5},{2,10},{6,14},... | collective-permute-start | bytes 20 | tf_op jit(solution)/shard_map/ppermute | solution.py:22
  16.2 18.0 %all-to-all-start.1 = ((bf16[4,1,64,576]{3,2,1,0:T(8,128)(2,1)}), bf16[4,1,64,576]{3,2,1,0:T(8,128)(2,1)S(1)}, u32[]{:S(2)}, u32[]{:S(2)}) async-start(bf16[4,1,64,576]{3,2,1,0:T(8,128)(2,1)} %bitcast.10), calls=%async_computation.1 | async-start | bytes 655360 | tf_op jit(solution)/shard_map/all_to_all | solution.py:61
  21.1 5.2 %collective-permute-start = (s32[1,1]{0,1:T(1,128)}, s32[1,1]{0,1:T(1,128)}, u32[]{:S(2)}, u32[]{:S(2)}) collective-permute-start(s32[1,1]{0,1:T(1,128)} %get-tuple-element.16), channel_id=1, source_target_pairs={{0,12},{4,0},{8,4},{12,8},{1,13},{5,1},{9,5},{13,9},{2,14},{6,2},{... | collective-permute-start | bytes 20 | tf_op jit(solution)/shard_map/ppermute | solution.py:22
  24.9 5.5 %collective-permute-start.2 = (s32[1,1]{0,1:T(1,128)}, s32[1,1]{0,1:T(1,128)}, u32[]{:S(2)}, u32[]{:S(2)}) collective-permute-start(s32[1,1]{0,1:T(1,128)} %get-tuple-element.18), channel_id=1, source_target_pairs={{0,4},{4,8},{8,12},{12,0},{1,5},{5,9},{9,13},{13,1},{2,6},{6,10},{... | collective-permute-start | bytes 20 | tf_op jit(solution)/shard_map/ppermute | solution.py:22
  24.9 5.5 %collective-permute-start.1 = (s32[1,1]{0,1:T(1,128)}, s32[1,1]{0,1:T(1,128)}, u32[]{:S(2)}, u32[]{:S(2)}) collective-permute-start(s32[1,1]{0,1:T(1,128)} %get-tuple-element.19), channel_id=1, source_target_pairs={{0,8},{4,12},{8,0},{12,4},{1,9},{5,13},{9,1},{13,5},{2,10},{6,14},... | collective-permute-start | bytes 20 | tf_op jit(solution)/shard_map/ppermute | solution.py:22
  34.2 11.5 %copy-start.1 = (bf16[4,1,64,576]{3,2,1,0:T(8,128)(2,1)}, bf16[4,1,64,576]{3,2,1,0:T(8,128)(2,1)S(1)}, u32[]{:S(2)}) copy-start(bf16[4,1,64,576]{3,2,1,0:T(8,128)(2,1)S(1)} %all-to-all-done.1) | copy-start | bytes 884740
  34.2 11.5 %all-to-all-start = ((bf16[4,1,64,576]{3,2,1,0:T(8,128)(2,1)}), bf16[4,1,64,576]{3,2,1,0:T(8,128)(2,1)S(1)}, u32[]{:S(2)}, u32[]{:S(2)}) async-start(bf16[4,1,64,576]{3,2,1,0:T(8,128)(2,1)} %bitcast.3), calls=%async_computation | async-start | bytes 655360 | tf_op jit(solution)/shard_map/all_to_all | solution.py:61
  45.7 0.8 copy-start.2
  46.5 53.1 %all-to-all-start.2 = ((bf16[128,128,128]{2,1,0:T(8,128)(2,1)}), bf16[128,128,128]{2,1,0:T(8,128)(2,1)}, u32[]{:S(2)}, u32[]{:S(2)}) async-start(bf16[128,128,128]{2,1,0:T(8,128)(2,1)} %param.9), calls=%async_computation.2 | async-start | bytes 8388608 | tf_op jit(solution)/shard_map/all_to_all | solution.py:76
  53.4 3.1 %copy-start.3 = (bf16[4,1,64,576]{3,2,1,0:T(8,128)(2,1)S(1)}, bf16[4,1,64,576]{3,2,1,0:T(8,128)(2,1)}, u32[]{:S(2)}) copy-start(bf16[4,1,64,576]{3,2,1,0:T(8,128)(2,1)} %copy-done.2) | copy-start | bytes 884740
  63.9 2.3 %copy-start.4 = (bf16[4,64,576]{2,1,0:T(8,128)(2,1)S(1)}, bf16[4,64,576]{2,1,0:T(8,128)(2,1)}, u32[]{:S(2)}) copy-start(bf16[4,64,576]{2,1,0:T(8,128)(2,1)} %gather_fusion.1) | copy-start | bytes 884740
  66.2 1.0 copy-start.5
